TPU v7x, 32 devices: a whole 2x2x4 slice. The times are simulated.
32 devices in a mesh: runs: 2 (over y), shot: 4 (over x, core), slab: 4 (over z).
Axes of the slice: x: 2, y: 2, z: 4, core: 2. Of those that a mesh axis runs over, the one named last changes fastest.
Arguments:
- source_now: float32 [16, 64, 16, 256], P(('runs', 'shot'), 'slab'), parts along dimension 0, may hold values from -4 to 4
- source_prev: float32 [16, 64, 16, 256], P(('runs', 'shot'), 'slab'), parts along dimension 0, may hold values from -4 to 4
- receiver_now: float32 [16, 64, 16, 256], P(('runs', 'shot'), 'slab'), parts along dimension 0, may hold values from -4 to 4
- receiver_prev: float32 [16, 64, 16, 256], P(('runs', 'shot'), 'slab'), parts along dimension 0, may hold values from -4 to 4
- courant_sq: float32 [128, 16, 256], P(('runs', 'slab')), parts along dimension 0, may hold values from 0.26 to 0.52
- source_cell: int32 [16], P(('runs', 'shot')), parts along dimension 0, may hold values from 0 to 1023
- wavelet: float32 [8, 16], P(None, ('runs', 'shot')), parts along dimension 1, may hold values from -12 to 12
- receiver_cell: int32 [16, 256], P(('runs', 'shot')), parts along dimension 0, may hold values from 0 to 1023
- traces: float32 [8, 16, 256], P(None, ('runs', 'shot')), parts along dimension 1, may hold values from -10 to 10
- offset_perm: int32 [16], P('runs'), parts along dimension 0, may hold values from 0 to 7, each once
Outputs:
- offset_image: float32 [16, 64, 16, 256], P(('runs', 'shot'), 'slab'), parts along dimension 0
- source_final: float32 [16, 64, 16, 256], P(('runs', 'shot'), 'slab'), parts along dimension 0
- receiver_final: float32 [16, 64, 16, 256], P(('runs', 'shot'), 'slab'), parts along dimension 0
There are 2 independent parts, one for each index of `runs`. A program takes and returns all parts, laid end to end along the dimension named above; each array names one. Nothing has to cross between parts.
Inputs may be any that keep to these rules, and one draw needn't show every extreme that they name: `source_cell`: a surface cell index. `receiver_cell`: surface cell indices; two receivers may share a cell. `offset_perm`: every offset index appears once.
All inputs are finite; a program needn't handle non-finite values.
Results may differ from a plain program's by a relative error of at most 0.0003.
Values sent between devices are 32-bit elements; how exact they have to be, the bound alone decides.
No kernel may reach another device: no remote copies, remote signals or barrier semaphores. Data moves between devices by JAX's collectives and lax.ppermute only.
A program may use at most 64 MiB of HBM per device.

v0:
```python
import jax
import jax.numpy as jnp
from jax import lax
from jax.sharding import PartitionSpec as P

OFF_DEV = 2
STEPS = 8
INJECT_Z = 4
stencil_weights = (-205.0 / 72.0, 8.0 / 5.0, -1.0 / 5.0, 8.0 / 315.0, -1.0 / 560.0)
side_weight = 1.0 / 16.0


def extended_2(cells, sides, width):
    for axis, dim in sides:
        count = lax.axis_size(axis)
        ends = count - 1
        head = lax.slice_in_dim(cells, 0, width, axis=dim)
        tail = lax.slice_in_dim(cells, cells.shape[dim] - width, cells.shape[dim], axis=dim)
        cells = jnp.concatenate(
            [
                lax.ppermute(tail, axis, [(i, (i + 1) % count) for i in range(ends)]),
                cells,
                lax.ppermute(head, axis, [((i + 1) % count, i) for i in range(ends)]),
            ],
            axis=dim,
        )
    return cells


def laplace_rows(extended):
    row_count = extended.shape[2] - 8
    centre = extended[:, :, 4 : 4 + row_count]
    size_y = centre.shape[3]
    size_z = centre.shape[4]
    padded = jnp.pad(centre, ((0, 0), (0, 0), (0, 0), (4, 4), (4, 4)))
    summed = (1.0 + 2.0 * side_weight) * stencil_weights[0] * centre
    for distance in range(1, 5):
        weight = stencil_weights[distance]
        summed = summed + weight * (
            extended[:, :, 4 + distance : 4 + distance + row_count]
            + extended[:, :, 4 - distance : 4 - distance + row_count]
        )
        summed = summed + side_weight * weight * (
            padded[:, :, :, 4 + distance : 4 + distance + size_y, 4 : 4 + size_z]
            + padded[:, :, :, 4 - distance : 4 - distance + size_y, 4 : 4 + size_z]
        )
        summed = summed + side_weight * weight * (
            padded[:, :, :, 4 : 4 + size_y, 4 + distance : 4 + distance + size_z]
            + padded[:, :, :, 4 : 4 + size_y, 4 - distance : 4 - distance + size_z]
        )
    return summed


def hot_tables(source_cell, receiver_cell, first_row, row_count, cells_y):
    positions = lax.broadcasted_iota(jnp.int32, (1, row_count * cells_y), 1) + first_row * cells_y
    source_hot = (source_cell[:, None] == positions).astype(jnp.float32)
    receiver_hot = (receiver_cell[:, :, None] == positions[None]).astype(jnp.float32)
    return (source_hot, receiver_hot)


def correlate(source_pad, receiver_pad, shift_by, half_span, extent):
    shifted_source = lax.dynamic_slice_in_dim(source_pad, half_span - shift_by, extent, axis=2)
    shifted_receiver = lax.dynamic_slice_in_dim(receiver_pad, half_span + shift_by, extent, axis=2)
    return jnp.sum(shifted_source * shifted_receiver, axis=0)


def body(
    source_now,
    source_prev,
    receiver_now,
    receiver_prev,
    courant_sq,
    source_cell,
    wavelet,
    receiver_cell,
    traces,
    offset_perm,
):
    shots_here, rows_here, cells_y, cells_z = source_now.shape
    slab_start = lax.axis_index("slab") * rows_here
    grid_rows = rows_here * lax.axis_size("slab")
    fields = jnp.stack([source_now, receiver_now])
    before = jnp.stack([source_prev, receiver_prev])
    local_tables = hot_tables(source_cell, receiver_cell, slab_start, rows_here, cells_y)
    for moment in range(STEPS):
        extended = extended_2(fields, (("slab", 2),), 4)
        row_count = extended.shape[2] - 8
        centre = extended[:, :, 4 : 4 + row_count]
        updated = 2.0 * centre - before + courant_sq * laplace_rows(extended)
        source_hot, receiver_hot = local_tables
        source_plane = source_hot * wavelet[moment][:, None]
        receiver_plane = jnp.einsum(
            "sr,src->sc", traces[moment], receiver_hot, precision=lax.Precision.HIGHEST
        )
        planes = jnp.stack([source_plane, receiver_plane]).reshape(
            2, shots_here, row_count, cells_y
        )
        updated = updated.at[:, :, :, :, INJECT_Z].add(planes)
        global_rows = slab_start + lax.broadcasted_iota(jnp.int32, (row_count,), 0)
        inside = (global_rows >= 0) & (global_rows < grid_rows)
        updated = jnp.where(inside[None, None, :, None, None], updated, 0.0)
        before, fields = (fields, updated)
    half_span = offset_perm.shape[0] // 2
    pad_widths = ((0, 0), (0, 0), (half_span, half_span), (0, 0))
    own_lags = lax.dynamic_slice_in_dim(offset_perm, lax.axis_index("shot") * OFF_DEV, OFF_DEV)
    shard_piece = lax.all_gather(fields, "shot", axis=1, tiled=True)
    source_pad = jnp.pad(shard_piece[0], pad_widths)
    receiver_pad = jnp.pad(shard_piece[1], pad_widths)
    products = [
        correlate(source_pad, receiver_pad, own_lags[slot_index] - half_span, half_span, cells_y)
        for slot_index in range(OFF_DEV)
    ]
    offset_image = jnp.stack(products)
    return (offset_image, fields[0], fields[1])


def solution(mesh):
    in_specs = (
        P(("runs", "shot"), "slab", None, None),
        P(("runs", "shot"), "slab", None, None),
        P(("runs", "shot"), "slab", None, None),
        P(("runs", "shot"), "slab", None, None),
        P(("runs", "slab"), None, None),
        P(("runs", "shot")),
        P(None, ("runs", "shot")),
        P(("runs", "shot"), None),
        P(None, ("runs", "shot"), None),
        P("runs"),
    )
    out_specs = (
        P(("runs", "shot"), "slab", None, None),
        P(("runs", "shot"), "slab", None, None),
        P(("runs", "shot"), "slab", None, None),
    )
    return jax.shard_map(body, mesh=mesh, in_specs=in_specs, out_specs=out_specs, check_vma=False)
```

profile of v0, /device:TPU:0, one launch (start us, length us, event | category | flops | bytes accessed | tf_op | source)
XLA Modules:
  0.0 271.8 jit_solution(146948616227826346)
XLA Ops:
  8.5 1.4 collective-permute-start
  9.9 5.6 %collective-permute-start.1 = (f32[2,2,4,16,256]{4,3,2,1,0:T(8,128)S(1)}, f32[2,2,4,16,256]{4,3,2,1,0:T(8,128)S(1)}, u32[]{:S(2)}, u32[]{:S(2)}) collective-permute-start(f32[2,2,4,16,256]{4,3,2,1,0:T(8,128)S(1)} %get-tuple-element.139), channel_id=1, source_target_pairs={{0,1},{1,2},{2,3},{4,5},{5,6},{6,7},{8,9},{9,10},{10,11},{12,13},{... | collective-permute-start | bytes 786440 | tf_op jit(solution)/shard_map/ppermute | solution.py:21
  17.8 2.1 collective-permute-done
  21.5 2.5 fusion.216
  25.1 5.3 %scatter-add.26 = f32[2,2,16,16,256]{4,3,2,1,0:T(8,128)S(1)} dynamic-update-slice(f32[2,2,16,16,256]{4,3,2,1,0:T(8,128)S(1)} %fusion.216, f32[2,2,16,16,1]{4,3,2,1,0:T(8,128)S(1)} %copy.241, s32[]{:T(128)} %constant.214.clone.1, s32[]{:T(128)} %constant.214.clone.1, s32[]{:T(128)} %constant.214.clone.1, s32[]{:T(128)} %constant.214.clone.1, s32[]{:T(128)} %constant.228.clone.1) | dynamic-update-slice | bytes 8196 | tf_op jit(solution)/shard_map/scatter-add | solution.py:98
  33.0 5.7 %collective-permute-start.3 = (f32[2,2,4,16,256]{4,3,2,1,0:T(8,128)S(1)}, f32[2,2,4,16,256]{4,3,2,1,0:T(8,128)}, u32[]{:S(2)}, u32[]{:S(2)}) collective-permute-start(f32[2,2,4,16,256]{4,3,2,1,0:T(8,128)S(1)} %get-tuple-element.135), channel_id=1, source_target_pairs={{0,1},{1,2},{2,3},{4,5},{5,6},{6,7},{8,9},{9,10},{10,11},{12,13},{... | collective-permute-start | bytes 786440 | tf_op jit(solution)/shard_map/ppermute | solution.py:21
  39.1 2.4 collective-permute-done.2
  42.7 14.2 %fusion.186 = f32[2,2,16,16,256]{4,3,2,1,0:T(8,128)S(1)} fusion(f32[2,2,16,16,256]{4,3,2,1,0:T(8,128)} %copy-done.10, f32[2,2,4,16,256]{4,3,2,1,0:T(8,128)} %collective-permute-done.3, f32[2,2,4,16,256]{4,3,2,1,0:T(8,128)} %copy-done.13, f32[16,16,256]{2,1,0:T(8,128)S(1)} %copy-done, f32[1,2,16,16,256]{4,3,2,1,0:T(8,128)S(1)} %bitcast.77, ...), kind=kLoop, calls=%fused_computation.411 | loop fusion | flops 13107200 | bytes 3932160 | tf_op jit(solution)/shard_map/add | solution.py:89
  58.0 6.7 %scatter-add.29 = f32[2,2,16,16,256]{4,3,2,1,0:T(8,128)} dynamic-update-slice(f32[2,2,16,16,256]{4,3,2,1,0:T(8,128)} %copy-done.5, f32[2,2,16,16,1]{4,3,2,1,0:T(8,128)S(1)} %copy.244, s32[]{:T(128)} %constant.214.clone.1, s32[]{:T(128)} %constant.214.clone.1, s32[]{:T(128)} %constant.214.clone.1, s32[]{:T(128)} %constant.214.clone.1, s32[]{:T(128)} %constant.228.clone.1) | dynamic-update-slice | bytes 8196 | tf_op jit(solution)/shard_map/scatter-add | solution.py:98
  64.8 1.4 broadcast_select_fusion.6
  67.5 5.1 %collective-permute-start.5 = (f32[2,2,4,16,256]{4,3,2,1,0:T(8,128)S(1)}, f32[2,2,4,16,256]{4,3,2,1,0:T(8,128)S(1)}, u32[]{:S(2)}, u32[]{:S(2)}) collective-permute-start(f32[2,2,4,16,256]{4,3,2,1,0:T(8,128)S(1)} %get-tuple-element.133), channel_id=1, source_target_pairs={{0,1},{1,2},{2,3},{4,5},{5,6},{6,7},{8,9},{9,10},{10,11},{12,13},{... | collective-permute-start | bytes 786440 | tf_op jit(solution)/shard_map/ppermute | solution.py:21
  73.1 2.2 collective-permute-done.4
  76.5 4.5 %fusion.160 = f32[2,2,16,16,256]{4,3,2,1,0:T(8,128)} fusion(f32[2,2,16,16,256]{4,3,2,1,0:T(8,128)S(1)} %broadcast_select_fusion.6, f32[2,2,4,16,256]{4,3,2,1,0:T(8,128)S(1)} %collective-permute-done.5, f32[2,2,4,16,256]{4,3,2,1,0:T(8,128)S(1)} %collective-permute-done.4, f32[16,16,256]{2,1,0:T(8,128)S(1)} %copy-done, ...), kind=kLoop, calls=%fused_computation.385 | loop fusion | flops 13107200 | bytes 3932176 | tf_op jit(solution)/shard_map/add | solution.py:89
  83.1 6.7 %scatter-add.30 = f32[2,2,16,16,256]{4,3,2,1,0:T(8,128)} dynamic-update-slice(f32[2,2,16,16,256]{4,3,2,1,0:T(8,128)} %fusion.160, f32[2,2,16,16,1]{4,3,2,1,0:T(8,128)S(1)} %copy.247, s32[]{:T(128)} %constant.214.clone.1, s32[]{:T(128)} %constant.214.clone.1, s32[]{:T(128)} %constant.214.clone.1, s32[]{:T(128)} %constant.214.clone.1, s32[]{:T(128)} %constant.228.clone.1) | dynamic-update-slice | bytes 8196 | tf_op jit(solution)/shard_map/scatter-add | solution.py:98
  89.9 1.4 broadcast_select_fusion.5
  92.7 5.2 %collective-permute-start.7 = (f32[2,2,4,16,256]{4,3,2,1,0:T(8,128)S(1)}, f32[2,2,4,16,256]{4,3,2,1,0:T(8,128)S(1)}, u32[]{:S(2)}, u32[]{:S(2)}) collective-permute-start(f32[2,2,4,16,256]{4,3,2,1,0:T(8,128)S(1)} %get-tuple-element.131), channel_id=1, source_target_pairs={{0,1},{1,2},{2,3},{4,5},{5,6},{6,7},{8,9},{9,10},{10,11},{12,13},{... | collective-permute-start | bytes 786440 | tf_op jit(solution)/shard_map/ppermute | solution.py:21
  98.3 1.8 collective-permute-done.6
  100.1 1.5 collective-permute-done.7
  101.5 4.5 %fusion.134 = f32[2,2,16,16,256]{4,3,2,1,0:T(8,128)} fusion(f32[2,2,16,16,256]{4,3,2,1,0:T(8,128)S(1)} %broadcast_select_fusion.5, f32[2,2,4,16,256]{4,3,2,1,0:T(8,128)S(1)} %collective-permute-done.7, f32[2,2,4,16,256]{4,3,2,1,0:T(8,128)S(1)} %collective-permute-done.6, f32[16,16,256]{2,1,0:T(8,128)S(1)} %copy-done, ...), kind=kLoop, calls=%fused_computation.359 | loop fusion | flops 13107200 | bytes 3932176 | tf_op jit(solution)/shard_map/add | solution.py:89
  108.2 6.7 %scatter-add.31 = f32[2,2,16,16,256]{4,3,2,1,0:T(8,128)} dynamic-update-slice(f32[2,2,16,16,256]{4,3,2,1,0:T(8,128)} %fusion.134, f32[2,2,16,16,1]{4,3,2,1,0:T(8,128)S(1)} %copy.250, s32[]{:T(128)} %constant.214.clone.1, s32[]{:T(128)} %constant.214.clone.1, s32[]{:T(128)} %constant.214.clone.1, s32[]{:T(128)} %constant.214.clone.1, s32[]{:T(128)} %constant.228.clone.1) | dynamic-update-slice | bytes 8196 | tf_op jit(solution)/shard_map/scatter-add | solution.py:98
  114.9 1.4 broadcast_select_fusion.4
  117.7 5.0 %collective-permute-start.9 = (f32[2,2,4,16,256]{4,3,2,1,0:T(8,128)S(1)}, f32[2,2,4,16,256]{4,3,2,1,0:T(8,128)S(1)}, u32[]{:S(2)}, u32[]{:S(2)}) collective-permute-start(f32[2,2,4,16,256]{4,3,2,1,0:T(8,128)S(1)} %get-tuple-element.129), channel_id=1, source_target_pairs={{0,1},{1,2},{2,3},{4,5},{5,6},{6,7},{8,9},{9,10},{10,11},{12,13},{... | collective-permute-start | bytes 786440 | tf_op jit(solution)/shard_map/ppermute | solution.py:21
  123.2 2.0 collective-permute-done.8
  125.1 1.5 collective-permute-done.9
  126.6 4.5 %fusion.108 = f32[2,2,16,16,256]{4,3,2,1,0:T(8,128)} fusion(f32[2,2,16,16,256]{4,3,2,1,0:T(8,128)S(1)} %broadcast_select_fusion.4, f32[2,2,4,16,256]{4,3,2,1,0:T(8,128)S(1)} %collective-permute-done.9, f32[2,2,4,16,256]{4,3,2,1,0:T(8,128)S(1)} %collective-permute-done.8, f32[16,16,256]{2,1,0:T(8,128)S(1)} %copy-done, ...), kind=kLoop, calls=%fused_computation.333 | loop fusion | flops 13107200 | bytes 3932176 | tf_op jit(solution)/shard_map/add | solution.py:89
  133.2 6.7 %scatter-add.34 = f32[2,2,16,16,256]{4,3,2,1,0:T(8,128)} dynamic-update-slice(f32[2,2,16,16,256]{4,3,2,1,0:T(8,128)} %fusion.108, f32[2,2,16,16,1]{4,3,2,1,0:T(8,128)S(1)} %copy.253, s32[]{:T(128)} %constant.214.clone.1, s32[]{:T(128)} %constant.214.clone.1, s32[]{:T(128)} %constant.214.clone.1, s32[]{:T(128)} %constant.214.clone.1, s32[]{:T(128)} %constant.228.clone.1) | dynamic-update-slice | bytes 8196 | tf_op jit(solution)/shard_map/scatter-add | solution.py:98
  140.0 1.4 broadcast_select_fusion.3
  142.7 5.0 %collective-permute-start.11 = (f32[2,2,4,16,256]{4,3,2,1,0:T(8,128)S(1)}, f32[2,2,4,16,256]{4,3,2,1,0:T(8,128)S(1)}, u32[]{:S(2)}, u32[]{:S(2)}) collective-permute-start(f32[2,2,4,16,256]{4,3,2,1,0:T(8,128)S(1)} %get-tuple-element.127), channel_id=1, source_target_pairs={{0,1},{1,2},{2,3},{4,5},{5,6},{6,7},{8,9},{9,10},{10,11},{12,13},{... | collective-permute-start | bytes 786440 | tf_op jit(solution)/shard_map/ppermute | solution.py:21
  148.2 2.0 collective-permute-done.10
  150.2 1.5 collective-permute-done.11
  151.6 4.5 %fusion.82 = f32[2,2,16,16,256]{4,3,2,1,0:T(8,128)} fusion(f32[2,2,16,16,256]{4,3,2,1,0:T(8,128)S(1)} %broadcast_select_fusion.3, f32[2,2,4,16,256]{4,3,2,1,0:T(8,128)S(1)} %collective-permute-done.11, f32[2,2,4,16,256]{4,3,2,1,0:T(8,128)S(1)} %collective-permute-done.10, f32[16,16,256]{2,1,0:T(8,128)S(1)} %copy-done, ...), kind=kLoop, calls=%fused_computation.307 | loop fusion | flops 13107200 | bytes 3932176 | tf_op jit(solution)/shard_map/add | solution.py:89
  158.3 6.7 %scatter-add.35 = f32[2,2,16,16,256]{4,3,2,1,0:T(8,128)} dynamic-update-slice(f32[2,2,16,16,256]{4,3,2,1,0:T(8,128)} %fusion.82, f32[2,2,16,16,1]{4,3,2,1,0:T(8,128)S(1)} %copy.256, s32[]{:T(128)} %constant.214.clone.1, s32[]{:T(128)} %constant.214.clone.1, s32[]{:T(128)} %constant.214.clone.1, s32[]{:T(128)} %constant.214.clone.1, s32[]{:T(128)} %constant.228.clone.1) | dynamic-update-slice | bytes 8196 | tf_op jit(solution)/shard_map/scatter-add | solution.py:98
  165.0 1.4 broadcast_select_fusion.2
  167.8 5.3 %collective-permute-start.13 = (f32[2,2,4,16,256]{4,3,2,1,0:T(8,128)S(1)}, f32[2,2,4,16,256]{4,3,2,1,0:T(8,128)S(1)}, u32[]{:S(2)}, u32[]{:S(2)}) collective-permute-start(f32[2,2,4,16,256]{4,3,2,1,0:T(8,128)S(1)} %get-tuple-element.125), channel_id=1, source_target_pairs={{0,1},{1,2},{2,3},{4,5},{5,6},{6,7},{8,9},{9,10},{10,11},{12,13},{... | collective-permute-start | bytes 786440 | tf_op jit(solution)/shard_map/ppermute | solution.py:21
  173.5 1.8 collective-permute-done.12
  175.2 1.5 collective-permute-done.13
  176.7 4.5 %fusion.56 = f32[2,2,16,16,256]{4,3,2,1,0:T(8,128)} fusion(f32[2,2,16,16,256]{4,3,2,1,0:T(8,128)S(1)} %broadcast_select_fusion.2, f32[2,2,4,16,256]{4,3,2,1,0:T(8,128)S(1)} %collective-permute-done.13, f32[2,2,4,16,256]{4,3,2,1,0:T(8,128)S(1)} %collective-permute-done.12, f32[16,16,256]{2,1,0:T(8,128)S(1)} %copy-done, ...), kind=kLoop, calls=%fused_computation.281 | loop fusion | flops 13107200 | bytes 3932176 | tf_op jit(solution)/shard_map/add | solution.py:89
  183.3 6.7 %scatter-add.36 = f32[2,2,16,16,256]{4,3,2,1,0:T(8,128)} dynamic-update-slice(f32[2,2,16,16,256]{4,3,2,1,0:T(8,128)} %fusion.56, f32[2,2,16,16,1]{4,3,2,1,0:T(8,128)S(1)} %copy.259, s32[]{:T(128)} %constant.214.clone.1, s32[]{:T(128)} %constant.214.clone.1, s32[]{:T(128)} %constant.214.clone.1, s32[]{:T(128)} %constant.214.clone.1, s32[]{:T(128)} %constant.228.clone.1) | dynamic-update-slice | bytes 8196 | tf_op jit(solution)/shard_map/scatter-add | solution.py:98
  190.0 1.4 broadcast_select_fusion.1
  192.8 5.0 %collective-permute-start.15 = (f32[2,2,4,16,256]{4,3,2,1,0:T(8,128)S(1)}, f32[2,2,4,16,256]{4,3,2,1,0:T(8,128)S(1)}, u32[]{:S(2)}, u32[]{:S(2)}) collective-permute-start(f32[2,2,4,16,256]{4,3,2,1,0:T(8,128)S(1)} %get-tuple-element.123), channel_id=1, source_target_pairs={{0,1},{1,2},{2,3},{4,5},{5,6},{6,7},{8,9},{9,10},{10,11},{12,13},{... | collective-permute-start | bytes 786440 | tf_op jit(solution)/shard_map/ppermute | solution.py:21
  198.3 2.0 collective-permute-done.14
  200.3 1.5 collective-permute-done.15
  201.7 4.5 %fusion.30 = f32[2,2,16,16,256]{4,3,2,1,0:T(8,128)} fusion(f32[2,2,16,16,256]{4,3,2,1,0:T(8,128)S(1)} %broadcast_select_fusion.1, f32[2,2,4,16,256]{4,3,2,1,0:T(8,128)S(1)} %collective-permute-done.15, f32[2,2,4,16,256]{4,3,2,1,0:T(8,128)S(1)} %collective-permute-done.14, f32[16,16,256]{2,1,0:T(8,128)S(1)} %copy-done, ...), kind=kLoop, calls=%fused_computation.255 | loop fusion | flops 13107200 | bytes 3932176 | tf_op jit(solution)/shard_map/add | solution.py:89
  208.4 6.7 %scatter-add.39 = f32[2,2,16,16,256]{4,3,2,1,0:T(8,128)} dynamic-update-slice(f32[2,2,16,16,256]{4,3,2,1,0:T(8,128)} %fusion.30, f32[2,2,16,16,1]{4,3,2,1,0:T(8,128)S(1)} %copy.262, s32[]{:T(128)} %constant.214.clone.1, s32[]{:T(128)} %constant.214.clone.1, s32[]{:T(128)} %constant.214.clone.1, s32[]{:T(128)} %constant.214.clone.1, s32[]{:T(128)} %constant.228.clone.1) | dynamic-update-slice | bytes 8196 | tf_op jit(solution)/shard_map/scatter-add | solution.py:98
  215.1 2.4 broadcast_select_fusion
  224.5 30.6 %all-gather.2.cloned.1.call-done = f32[2,8,16,16,256]{4,3,2,1,0:T(8,128)} async-done(((f32[2,2,16,16,256]{4,3,2,1,0:T(8,128)}), f32[2,8,16,16,256]{4,3,2,1,0:T(8,128)}) %all-gather.2.cloned.1.call-update) | async-done | bytes 4194320 | tf_op jit(solution)/shard_map/all_gather | solution.py:106
  255.1 2.7 slice_bitcast_fusion
  257.7 1.8 fusion.1
  (151 shorter events, 42.9 us)
Async XLA Ops:
  7.2 8.4 %copy-start.9 = (f32[2,16,16,256]{3,2,1,0:T(8,128)S(1)}, f32[2,16,16,256]{3,2,1,0:T(8,128)}, u32[]{:S(2)}) copy-start(f32[2,16,16,256]{3,2,1,0:T(8,128)} %param.26) | copy-start | bytes 1572868
  7.2 8.4 %copy-start.8 = (f32[2,16,16,256]{3,2,1,0:T(8,128)S(1)}, f32[2,16,16,256]{3,2,1,0:T(8,128)}, u32[]{:S(2)}) copy-start(f32[2,16,16,256]{3,2,1,0:T(8,128)} %param.28) | copy-start | bytes 1572868
  7.2 247.9 %all-gather.2.cloned.1.call-start = ((), (), s32[]{:S(2)}) async-start(), calls=%async_computation | async-start | bytes 5242880 | tf_op jit(solution)/shard_map/all_gather | solution.py:106
  8.5 7.2 %copy-start.14 = (f32[8,2]{0,1:T(2,128)S(1)}, f32[8,2]{0,1:T(2,128)}, u32[]{:S(2)}) copy-start(f32[8,2]{0,1:T(2,128)} %param.32) | copy-start | bytes 196
  8.5 7.5 %copy-start.16 = (f32[8,2,256]{2,1,0:T(2,128)S(1)}, f32[8,2,256]{2,1,0:T(2,128)}, u32[]{:S(2)}) copy-start(f32[8,2,256]{2,1,0:T(2,128)} %param.34) | copy-start | bytes 49156
  8.5 8.1 %copy-start.22 = (s32[2,256]{1,0:T(2,128)S(1)}, s32[2,256]{1,0:T(2,128)}, u32[]{:S(2)}) copy-start(s32[2,256]{1,0:T(2,128)} %param.33) | copy-start | bytes 6148
  8.5 9.2 %copy-start.21 = (s32[2]{0:T(128)S(1)}, s32[2]{0:T(128)}, u32[]{:S(2)}) copy-start(s32[2]{0:T(128)} %param.31) | copy-start | bytes 28
  8.5 11.4 %collective-permute-start = (f32[2,2,4,16,256]{4,3,2,1,0:T(8,128)S(1)}, f32[2,2,4,16,256]{4,3,2,1,0:T(8,128)S(1)}, u32[]{:S(2)}, u32[]{:S(2)}) collective-permute-start(f32[2,2,4,16,256]{4,3,2,1,0:T(8,128)S(1)} %get-tuple-element.138), channel_id=1, source_target_pairs={{1,0},{2,1},{3,2},{5,4},{6,5},{7,6},{9,8},{10,9},{11,10},{13,12},{... | collective-permute-start | bytes 786440 | tf_op jit(solution)/shard_map/ppermute | solution.py:23
  9.9 11.1 %collective-permute-start.1 = (f32[2,2,4,16,256]{4,3,2,1,0:T(8,128)S(1)}, f32[2,2,4,16,256]{4,3,2,1,0:T(8,128)S(1)}, u32[]{:S(2)}, u32[]{:S(2)}) collective-permute-start(f32[2,2,4,16,256]{4,3,2,1,0:T(8,128)S(1)} %get-tuple-element.139), channel_id=1, source_target_pairs={{0,1},{1,2},{2,3},{4,5},{5,6},{6,7},{8,9},{9,10},{10,11},{12,13},{... | collective-permute-start | bytes 786440 | tf_op jit(solution)/shard_map/ppermute | solution.py:21
  15.7 2.0 copy-start.26
  17.7 3.7 %copy-start = (f32[16,16,256]{2,1,0:T(8,128)S(1)}, f32[16,16,256]{2,1,0:T(8,128)}, u32[]{:S(2)}) copy-start(f32[16,16,256]{2,1,0:T(8,128)} %param.30) | copy-start | bytes 786436
  17.8 3.7 %copy-start.11 = (f32[2,16,16,256]{3,2,1,0:T(8,128)S(1)}, f32[2,16,16,256]{3,2,1,0:T(8,128)}, u32[]{:S(2)}) copy-start(f32[2,16,16,256]{3,2,1,0:T(8,128)} %param.29) | copy-start | bytes 1572868
  17.8 3.7 %copy-start.12 = (f32[2,16,16,256]{3,2,1,0:T(8,128)S(1)}, f32[2,16,16,256]{3,2,1,0:T(8,128)}, u32[]{:S(2)}) copy-start(f32[2,16,16,256]{3,2,1,0:T(8,128)} %param.27) | copy-start | bytes 1572868
  23.9 0.7 copy-start.15
  30.5 8.2 %copy-start.20 = (f32[2,256,1]{1,0,2:T(2,128)S(1)}, f32[2,256,1]{1,0,2:T(2,128)}, u32[]{:S(2)}) copy-start(f32[2,256,1]{1,0,2:T(2,128)} %get-tuple-element.145) | copy-start | bytes 6148
  30.5 8.2 %copy-start.23 = (s32[2,256]{1,0:T(2,128)S(1)}, s32[2,256]{1,0:T(2,128)}, u32[]{:S(2)}) copy-start(s32[2,256]{1,0:T(2,128)} %param.33) | copy-start | bytes 6148
  30.5 8.2 %copy-start.27 = (s32[256]{0:T(256)S(1)}, s32[256]{0:T(256)}, u32[]{:S(2)}) copy-start(s32[256]{0:T(256)} %copy-done.26) | copy-start | bytes 3076
  30.6 1.0 copy-start.10
  31.7 9.8 %collective-permute-start.2 = (f32[2,2,4,16,256]{4,3,2,1,0:T(8,128)S(1)}, f32[2,2,4,16,256]{4,3,2,1,0:T(8,128)S(1)}, u32[]{:S(2)}, u32[]{:S(2)}) collective-permute-start(f32[2,2,4,16,256]{4,3,2,1,0:T(8,128)S(1)} %get-tuple-element.134), channel_id=1, source_target_pairs={{1,0},{2,1},{3,2},{5,4},{6,5},{7,6},{9,8},{10,9},{11,10},{13,12},{... | collective-permute-start | bytes 786440 | tf_op jit(solution)/shard_map/ppermute | solution.py:23
  33.0 9.7 %collective-permute-start.3 = (f32[2,2,4,16,256]{4,3,2,1,0:T(8,128)S(1)}, f32[2,2,4,16,256]{4,3,2,1,0:T(8,128)}, u32[]{:S(2)}, u32[]{:S(2)}) collective-permute-start(f32[2,2,4,16,256]{4,3,2,1,0:T(8,128)S(1)} %get-tuple-element.135), channel_id=1, source_target_pairs={{0,1},{1,2},{2,3},{4,5},{5,6},{6,7},{8,9},{9,10},{10,11},{12,13},{... | collective-permute-start | bytes 786440 | tf_op jit(solution)/shard_map/ppermute | solution.py:21
  41.5 0.7 copy-start.13
  56.9 1.1 copy-start.5
  64.8 7.9 %copy-start.19 = (f32[2,256,1]{1,0,2:T(2,128)S(1)}, f32[2,256,1]{1,0,2:T(2,128)}, u32[]{:S(2)}) copy-start(f32[2,256,1]{1,0,2:T(2,128)} %get-tuple-element.144) | copy-start | bytes 6148
  64.8 7.9 %copy-start.24 = (s32[2,256]{1,0:T(2,128)S(1)}, s32[2,256]{1,0:T(2,128)}, u32[]{:S(2)}) copy-start(s32[2,256]{1,0:T(2,128)} %param.33) | copy-start | bytes 6148
  64.8 7.9 %copy-start.28 = (s32[256]{0:T(256)S(1)}, s32[256]{0:T(256)}, u32[]{:S(2)}) copy-start(s32[256]{0:T(256)} %copy-done.26) | copy-start | bytes 3076
  66.2 9.1 %collective-permute-start.4 = (f32[2,2,4,16,256]{4,3,2,1,0:T(8,128)S(1)}, f32[2,2,4,16,256]{4,3,2,1,0:T(8,128)S(1)}, u32[]{:S(2)}, u32[]{:S(2)}) collective-permute-start(f32[2,2,4,16,256]{4,3,2,1,0:T(8,128)S(1)} %get-tuple-element.132), channel_id=1, source_target_pairs={{1,0},{2,1},{3,2},{5,4},{6,5},{7,6},{9,8},{10,9},{11,10},{13,12},{... | collective-permute-start | bytes 786440 | tf_op jit(solution)/shard_map/ppermute | solution.py:23
  67.5 9.0 %collective-permute-start.5 = (f32[2,2,4,16,256]{4,3,2,1,0:T(8,128)S(1)}, f32[2,2,4,16,256]{4,3,2,1,0:T(8,128)S(1)}, u32[]{:S(2)}, u32[]{:S(2)}) collective-permute-start(f32[2,2,4,16,256]{4,3,2,1,0:T(8,128)S(1)} %get-tuple-element.133), channel_id=1, source_target_pairs={{0,1},{1,2},{2,3},{4,5},{5,6},{6,7},{8,9},{9,10},{10,11},{12,13},{... | collective-permute-start | bytes 786440 | tf_op jit(solution)/shard_map/ppermute | solution.py:21
  89.8 8.0 %copy-start.18 = (f32[2,256,1]{1,0,2:T(2,128)S(1)}, f32[2,256,1]{1,0,2:T(2,128)}, u32[]{:S(2)}) copy-start(f32[2,256,1]{1,0,2:T(2,128)} %get-tuple-element.143) | copy-start | bytes 6148
  89.9 11.7 %copy-start.6 = (f32[2,2,16,16,256]{4,3,2,1,0:T(8,128)S(1)}, f32[2,2,16,16,256]{4,3,2,1,0:T(8,128)}, u32[]{:S(2)}) copy-start(f32[2,2,16,16,256]{4,3,2,1,0:T(8,128)} %scatter-add.29) | copy-start | bytes 3145732
  91.4 8.7 %collective-permute-start.6 = (f32[2,2,4,16,256]{4,3,2,1,0:T(8,128)S(1)}, f32[2,2,4,16,256]{4,3,2,1,0:T(8,128)S(1)}, u32[]{:S(2)}, u32[]{:S(2)}) collective-permute-start(f32[2,2,4,16,256]{4,3,2,1,0:T(8,128)S(1)} %get-tuple-element.130), channel_id=1, source_target_pairs={{1,0},{2,1},{3,2},{5,4},{6,5},{7,6},{9,8},{10,9},{11,10},{13,12},{... | collective-permute-start | bytes 786440 | tf_op jit(solution)/shard_map/ppermute | solution.py:23
  92.7 8.9 %collective-permute-start.7 = (f32[2,2,4,16,256]{4,3,2,1,0:T(8,128)S(1)}, f32[2,2,4,16,256]{4,3,2,1,0:T(8,128)S(1)}, u32[]{:S(2)}, u32[]{:S(2)}) collective-permute-start(f32[2,2,4,16,256]{4,3,2,1,0:T(8,128)S(1)} %get-tuple-element.131), channel_id=1, source_target_pairs={{0,1},{1,2},{2,3},{4,5},{5,6},{6,7},{8,9},{9,10},{10,11},{12,13},{... | collective-permute-start | bytes 786440 | tf_op jit(solution)/shard_map/ppermute | solution.py:21
  114.9 7.8 %copy-start.17 = (f32[2,256,1]{1,0,2:T(2,128)S(1)}, f32[2,256,1]{1,0,2:T(2,128)}, u32[]{:S(2)}) copy-start(f32[2,256,1]{1,0,2:T(2,128)} %get-tuple-element.142) | copy-start | bytes 6148
  114.9 11.7 %copy-start.1 = (f32[2,2,16,16,256]{4,3,2,1,0:T(8,128)S(1)}, f32[2,2,16,16,256]{4,3,2,1,0:T(8,128)}, u32[]{:S(2)}) copy-start(f32[2,2,16,16,256]{4,3,2,1,0:T(8,128)} %scatter-add.30) | copy-start | bytes 3145732
  116.4 8.7 %collective-permute-start.8 = (f32[2,2,4,16,256]{4,3,2,1,0:T(8,128)S(1)}, f32[2,2,4,16,256]{4,3,2,1,0:T(8,128)S(1)}, u32[]{:S(2)}, u32[]{:S(2)}) collective-permute-start(f32[2,2,4,16,256]{4,3,2,1,0:T(8,128)S(1)} %get-tuple-element.128), channel_id=1, source_target_pairs={{1,0},{2,1},{3,2},{5,4},{6,5},{7,6},{9,8},{10,9},{11,10},{13,12},{... | collective-permute-start | bytes 786440 | tf_op jit(solution)/shard_map/ppermute | solution.py:23
  117.7 8.9 %collective-permute-start.9 = (f32[2,2,4,16,256]{4,3,2,1,0:T(8,128)S(1)}, f32[2,2,4,16,256]{4,3,2,1,0:T(8,128)S(1)}, u32[]{:S(2)}, u32[]{:S(2)}) collective-permute-start(f32[2,2,4,16,256]{4,3,2,1,0:T(8,128)S(1)} %get-tuple-element.129), channel_id=1, source_target_pairs={{0,1},{1,2},{2,3},{4,5},{5,6},{6,7},{8,9},{9,10},{10,11},{12,13},{... | collective-permute-start | bytes 786440 | tf_op jit(solution)/shard_map/ppermute | solution.py:21
  139.9 11.7 %copy-start.2 = (f32[2,2,16,16,256]{4,3,2,1,0:T(8,128)S(1)}, f32[2,2,16,16,256]{4,3,2,1,0:T(8,128)}, u32[]{:S(2)}) copy-start(f32[2,2,16,16,256]{4,3,2,1,0:T(8,128)} %scatter-add.31) | copy-start | bytes 3145732
  141.4 8.7 %collective-permute-start.10 = (f32[2,2,4,16,256]{4,3,2,1,0:T(8,128)S(1)}, f32[2,2,4,16,256]{4,3,2,1,0:T(8,128)S(1)}, u32[]{:S(2)}, u32[]{:S(2)}) collective-permute-start(f32[2,2,4,16,256]{4,3,2,1,0:T(8,128)S(1)} %get-tuple-element.126), channel_id=1, source_target_pairs={{1,0},{2,1},{3,2},{5,4},{6,5},{7,6},{9,8},{10,9},{11,10},{13,12},{... | collective-permute-start | bytes 786440 | tf_op jit(solution)/shard_map/ppermute | solution.py:23
  142.7 8.9 %collective-permute-start.11 = (f32[2,2,4,16,256]{4,3,2,1,0:T(8,128)S(1)}, f32[2,2,4,16,256]{4,3,2,1,0:T(8,128)S(1)}, u32[]{:S(2)}, u32[]{:S(2)}) collective-permute-start(f32[2,2,4,16,256]{4,3,2,1,0:T(8,128)S(1)} %get-tuple-element.127), channel_id=1, source_target_pairs={{0,1},{1,2},{2,3},{4,5},{5,6},{6,7},{8,9},{9,10},{10,11},{12,13},{... | collective-permute-start | bytes 786440 | tf_op jit(solution)/shard_map/ppermute | solution.py:21
  165.0 11.7 %copy-start.3 = (f32[2,2,16,16,256]{4,3,2,1,0:T(8,128)S(1)}, f32[2,2,16,16,256]{4,3,2,1,0:T(8,128)}, u32[]{:S(2)}) copy-start(f32[2,2,16,16,256]{4,3,2,1,0:T(8,128)} %scatter-add.34) | copy-start | bytes 3145732
  166.5 8.7 %collective-permute-start.12 = (f32[2,2,4,16,256]{4,3,2,1,0:T(8,128)S(1)}, f32[2,2,4,16,256]{4,3,2,1,0:T(8,128)S(1)}, u32[]{:S(2)}, u32[]{:S(2)}) collective-permute-start(f32[2,2,4,16,256]{4,3,2,1,0:T(8,128)S(1)} %get-tuple-element.124), channel_id=1, source_target_pairs={{1,0},{2,1},{3,2},{5,4},{6,5},{7,6},{9,8},{10,9},{11,10},{13,12},{... | collective-permute-start | bytes 786440 | tf_op jit(solution)/shard_map/ppermute | solution.py:23
  167.8 8.9 %collective-permute-start.13 = (f32[2,2,4,16,256]{4,3,2,1,0:T(8,128)S(1)}, f32[2,2,4,16,256]{4,3,2,1,0:T(8,128)S(1)}, u32[]{:S(2)}, u32[]{:S(2)}) collective-permute-start(f32[2,2,4,16,256]{4,3,2,1,0:T(8,128)S(1)} %get-tuple-element.125), channel_id=1, source_target_pairs={{0,1},{1,2},{2,3},{4,5},{5,6},{6,7},{8,9},{9,10},{10,11},{12,13},{... | collective-permute-start | bytes 786440 | tf_op jit(solution)/shard_map/ppermute | solution.py:21
  190.0 11.7 %copy-start.4 = (f32[2,2,16,16,256]{4,3,2,1,0:T(8,128)S(1)}, f32[2,2,16,16,256]{4,3,2,1,0:T(8,128)}, u32[]{:S(2)}) copy-start(f32[2,2,16,16,256]{4,3,2,1,0:T(8,128)} %scatter-add.35) | copy-start | bytes 3145732
  191.5 8.7 %collective-permute-start.14 = (f32[2,2,4,16,256]{4,3,2,1,0:T(8,128)S(1)}, f32[2,2,4,16,256]{4,3,2,1,0:T(8,128)S(1)}, u32[]{:S(2)}, u32[]{:S(2)}) collective-permute-start(f32[2,2,4,16,256]{4,3,2,1,0:T(8,128)S(1)} %get-tuple-element.122), channel_id=1, source_target_pairs={{1,0},{2,1},{3,2},{5,4},{6,5},{7,6},{9,8},{10,9},{11,10},{13,12},{... | collective-permute-start | bytes 786440 | tf_op jit(solution)/shard_map/ppermute | solution.py:23
  192.8 8.9 %collective-permute-start.15 = (f32[2,2,4,16,256]{4,3,2,1,0:T(8,128)S(1)}, f32[2,2,4,16,256]{4,3,2,1,0:T(8,128)S(1)}, u32[]{:S(2)}, u32[]{:S(2)}) collective-permute-start(f32[2,2,4,16,256]{4,3,2,1,0:T(8,128)S(1)} %get-tuple-element.123), channel_id=1, source_target_pairs={{0,1},{1,2},{2,3},{4,5},{5,6},{6,7},{8,9},{9,10},{10,11},{12,13},{... | collective-permute-start | bytes 786440 | tf_op jit(solution)/shard_map/ppermute | solution.py:21
  215.1 2.4 copy-start.25
  217.5 5.9 %copy-start.7 = (f32[2,2,16,16,256]{4,3,2,1,0:T(8,128)S(1)}, f32[2,2,16,16,256]{4,3,2,1,0:T(8,128)}, u32[]{:S(2)}) copy-start(f32[2,2,16,16,256]{4,3,2,1,0:T(8,128)} %broadcast_select_fusion) | copy-start | bytes 3145732
Sparse Core Ops, SparseCore 0:
  217.7 37.3 all-gather.1
where the time goes:
time: 273 us; the launch traced here: 272 us
  local copies, waits for them, and re-layouts  80.7 us (30%)
  other arithmetic  59.1 us (22%)
  waiting for transfers between devices  57 us (21%)
  starting transfers between devices  52.5 us (19%)
  between operations  19.9 us (7%)
    scatter-add x8, local copies, waits for them, and re-layouts, body(): updated = updated.at[:, :, :, :, INJECT_Z].add(planes)  52.5 us
    add x8, other arithmetic, body(): updated = 2.0 * centre - before + courant_sq * laplace_rows(extended)  43.4 us
    ppermute x8, starting transfers between devices, extended_2(): lax.ppermute(tail, axis, [(i, (i + 1) % count) for i in range(ends)])  42 us
    all_gather x1, waiting for transfers between devices, body(): shard_piece = lax.all_gather(fields, 'shot', axis=1, tiled=True)  30.6 us
    ppermute x8, waiting for transfers between devices, extended_2(): lax.ppermute(head, axis, [((i + 1) % count, i) for i in range(ends)])  16.2 us
    another operation x16, local copies, waits for them, and re-layouts  11.3 us
    select_n x8, other arithmetic, body(): updated = jnp.where(inside[None, None, :, None, None], updated, 0.0)  11.2 us
    ppermute x8, starting transfers between devices, extended_2(): lax.ppermute(head, axis, [((i + 1) % count, i) for i in range(ends)])  10.5 us
  transfers between devices with their start and end apart: 17, of which 17 were waited for; matrix products, arithmetic and copies ran while one was open for 2% of the time, Pallas kernels for 0%

commit v1 on v0

--- a/solution.py
+++ b/solution.py
@@ -103,7 +103,19 @@
     half_span = offset_perm.shape[0] // 2
     pad_widths = ((0, 0), (0, 0), (half_span, half_span), (0, 0))
     own_lags = lax.dynamic_slice_in_dim(offset_perm, lax.axis_index("shot") * OFF_DEV, OFF_DEV)
-    shard_piece = lax.all_gather(fields, "shot", axis=1, tiled=True)
+    n_axis = lax.psum(1, "shot")
+    rack = [(hop_no, (hop_no + 1) % n_axis) for hop_no in range(n_axis)]
+    views = [(hop_no, (hop_no - 1) % n_axis) for hop_no in range(n_axis)]
+    current_value, u1 = ([fields], [fields])
+    for _ in range(n_axis // 2):
+        placed = lax.ppermute(current_value[-1], "shot", rack)
+        current_value.append(placed)
+    for _ in range((n_axis - 1) // 2):
+        p_next = lax.ppermute(u1[-1], "shot", perm=views)
+        u1.append(p_next)
+    heard = jnp.concatenate([*current_value[::-1], *u1[1:]], axis=1)
+    near = lax.axis_index("shot")
+    shard_piece = jnp.roll(heard, (near - n_axis // 2) * fields.shape[1], axis=1)
     source_pad = jnp.pad(shard_piece[0], pad_widths)
     receiver_pad = jnp.pad(shard_piece[1], pad_widths)
     products = [

time: 273 us -> 262 us (0.960)
  between operations: 19.9 us -> 6.62 us
    all_gather x1 -> x0, waiting for transfers between devices: 30.6 us -> none  [body(): shard_piece = lax.all_gather(fields, 'shot', axis=1, tiled=True)]
    ppermute x0 -> x3, waiting for transfers between devices: none -> 29.5 us  [the longest x2 29.5 us: body(): placed = lax.ppermute(current_value[-1], 'shot', rack)]
    unnamed x60 -> x63, local copies, waits for them, and re-layouts: 4.44 us -> 7.16 us
  transfers between devices with their start and end apart: 17 -> 19, of which waited for: 17 -> 18; matrix products, arithmetic and copies ran while one was open for 2% -> 4% of each run, Pallas kernels for 0% -> 0%
where the time goes in v1:
time: 262 us; the launch traced here: 260 us
  local copies, waits for them, and re-layouts  81.9 us (31%)
  other arithmetic  59.7 us (23%)
  waiting for transfers between devices  54.6 us (21%)
  starting transfers between devices  54.1 us (21%)
  between operations  6.62 us (3%)
    scatter-add x8, local copies, waits for them, and re-layouts, body(): updated = updated.at[:, :, :, :, INJECT_Z].add(planes)  53 us
    add x8, other arithmetic, body(): updated = 2.0 * centre - before + courant_sq * laplace_rows(extended)  43.4 us
    ppermute x8, starting transfers between devices, extended_2(): lax.ppermute(tail, axis, [(i, (i + 1) % count) for i in range(ends)])  42 us
    ppermute x2, waiting for transfers between devices, body(): placed = lax.ppermute(current_value[-1], 'shot', rack)  29.5 us
    ppermute x8, waiting for transfers between devices, extended_2(): lax.ppermute(head, axis, [((i + 1) % count, i) for i in range(ends)])  15 us
    another operation x16, local copies, waits for them, and re-layouts  11.3 us
    ppermute x8, starting transfers between devices, extended_2(): lax.ppermute(head, axis, [((i + 1) % count, i) for i in range(ends)])  10.3 us
    ppermute x8, waiting for transfers between devices, extended_2(): lax.ppermute(tail, axis, [(i, (i + 1) % count) for i in range(ends)])  10.2 us
  transfers between devices with their start and end apart: 19, of which 18 were waited for; matrix products, arithmetic and copies ran while one was open for 4% of the time, Pallas kernels for 0%

profile of v1, /device:TPU:0, one launch (start us, length us, event | category | flops | bytes accessed | tf_op | source)
XLA Modules:
  0.0 259.7 jit_solution(9029449336668220096)
XLA Ops:
  3.2 5.6 %collective-permute-start.1 = (f32[2,2,4,16,256]{4,3,2,1,0:T(8,128)S(1)}, f32[2,2,4,16,256]{4,3,2,1,0:T(8,128)S(1)}, u32[]{:S(2)}, u32[]{:S(2)}) collective-permute-start(f32[2,2,4,16,256]{4,3,2,1,0:T(8,128)S(1)} %get-tuple-element.139), channel_id=1, source_target_pairs={{0,1},{1,2},{2,3},{4,5},{5,6},{6,7},{8,9},{9,10},{10,11},{12,13},{... | collective-permute-start | bytes 786440 | tf_op jit(solution)/shard_map/ppermute | solution.py:21
  14.7 2.5 fusion.216
  19.1 5.4 %scatter-add.26 = f32[2,2,16,16,256]{4,3,2,1,0:T(8,128)S(1)} dynamic-update-slice(f32[2,2,16,16,256]{4,3,2,1,0:T(8,128)S(1)} %fusion.216, f32[2,2,16,16,1]{4,3,2,1,0:T(8,128)S(1)} %copy.253, s32[]{:T(128)} %constant.233.clone.1, s32[]{:T(128)} %constant.233.clone.1, s32[]{:T(128)} %constant.233.clone.1, s32[]{:T(128)} %constant.233.clone.1, s32[]{:T(128)} %constant.247.clone.1) | dynamic-update-slice | bytes 8196 | tf_op jit(solution)/shard_map/scatter-add | solution.py:98
  26.9 5.7 %collective-permute-start.3 = (f32[2,2,4,16,256]{4,3,2,1,0:T(8,128)S(1)}, f32[2,2,4,16,256]{4,3,2,1,0:T(8,128)}, u32[]{:S(2)}, u32[]{:S(2)}) collective-permute-start(f32[2,2,4,16,256]{4,3,2,1,0:T(8,128)S(1)} %get-tuple-element.135), channel_id=1, source_target_pairs={{0,1},{1,2},{2,3},{4,5},{5,6},{6,7},{8,9},{9,10},{10,11},{12,13},{... | collective-permute-start | bytes 786440 | tf_op jit(solution)/shard_map/ppermute | solution.py:21
  33.0 2.4 collective-permute-done.2
  36.6 14.1 %fusion.186 = f32[2,2,16,16,256]{4,3,2,1,0:T(8,128)S(1)} fusion(f32[2,2,16,16,256]{4,3,2,1,0:T(8,128)} %copy-done.10, f32[2,2,4,16,256]{4,3,2,1,0:T(8,128)} %collective-permute-done.3, f32[2,2,4,16,256]{4,3,2,1,0:T(8,128)} %copy-done.13, f32[16,16,256]{2,1,0:T(8,128)S(1)} %copy-done.1, f32[1,2,16,16,256]{4,3,2,1,0:T(8,128)S(1)} %bitcast.77, ...), kind=kLoop, calls=%fused_computation.411 | loop fusion | flops 13107200 | bytes 3932160 | tf_op jit(solution)/shard_map/add | solution.py:89
  51.9 6.8 %scatter-add.29 = f32[2,2,16,16,256]{4,3,2,1,0:T(8,128)} dynamic-update-slice(f32[2,2,16,16,256]{4,3,2,1,0:T(8,128)} %copy-done.6, f32[2,2,16,16,1]{4,3,2,1,0:T(8,128)S(1)} %copy.256, s32[]{:T(128)} %constant.233.clone.1, s32[]{:T(128)} %constant.233.clone.1, s32[]{:T(128)} %constant.233.clone.1, s32[]{:T(128)} %constant.233.clone.1, s32[]{:T(128)} %constant.247.clone.1) | dynamic-update-slice | bytes 8196 | tf_op jit(solution)/shard_map/scatter-add | solution.py:98
  58.6 1.4 broadcast_select_fusion.6
  61.3 5.1 %collective-permute-start.5 = (f32[2,2,4,16,256]{4,3,2,1,0:T(8,128)S(1)}, f32[2,2,4,16,256]{4,3,2,1,0:T(8,128)S(1)}, u32[]{:S(2)}, u32[]{:S(2)}) collective-permute-start(f32[2,2,4,16,256]{4,3,2,1,0:T(8,128)S(1)} %get-tuple-element.133), channel_id=1, source_target_pairs={{0,1},{1,2},{2,3},{4,5},{5,6},{6,7},{8,9},{9,10},{10,11},{12,13},{... | collective-permute-start | bytes 786440 | tf_op jit(solution)/shard_map/ppermute | solution.py:21
  66.9 2.2 collective-permute-done.4
  70.3 4.5 %fusion.160 = f32[2,2,16,16,256]{4,3,2,1,0:T(8,128)} fusion(f32[2,2,16,16,256]{4,3,2,1,0:T(8,128)S(1)} %broadcast_select_fusion.6, f32[2,2,4,16,256]{4,3,2,1,0:T(8,128)S(1)} %collective-permute-done.5, f32[2,2,4,16,256]{4,3,2,1,0:T(8,128)S(1)} %collective-permute-done.4, f32[16,16,256]{2,1,0:T(8,128)S(1)} %copy-done.1, ...), kind=kLoop, calls=%fused_computation.385 | loop fusion | flops 13107200 | bytes 3932176 | tf_op jit(solution)/shard_map/add | solution.py:89
  77.0 6.8 %scatter-add.30 = f32[2,2,16,16,256]{4,3,2,1,0:T(8,128)} dynamic-update-slice(f32[2,2,16,16,256]{4,3,2,1,0:T(8,128)} %fusion.160, f32[2,2,16,16,1]{4,3,2,1,0:T(8,128)S(1)} %copy.259, s32[]{:T(128)} %constant.233.clone.1, s32[]{:T(128)} %constant.233.clone.1, s32[]{:T(128)} %constant.233.clone.1, s32[]{:T(128)} %constant.233.clone.1, s32[]{:T(128)} %constant.247.clone.1) | dynamic-update-slice | bytes 8196 | tf_op jit(solution)/shard_map/scatter-add | solution.py:98
  83.8 1.4 broadcast_select_fusion.5
  86.5 5.2 %collective-permute-start.7 = (f32[2,2,4,16,256]{4,3,2,1,0:T(8,128)S(1)}, f32[2,2,4,16,256]{4,3,2,1,0:T(8,128)S(1)}, u32[]{:S(2)}, u32[]{:S(2)}) collective-permute-start(f32[2,2,4,16,256]{4,3,2,1,0:T(8,128)S(1)} %get-tuple-element.131), channel_id=1, source_target_pairs={{0,1},{1,2},{2,3},{4,5},{5,6},{6,7},{8,9},{9,10},{10,11},{12,13},{... | collective-permute-start | bytes 786440 | tf_op jit(solution)/shard_map/ppermute | solution.py:21
  92.2 1.8 collective-permute-done.6
  94.0 1.5 collective-permute-done.7
  95.4 4.5 %fusion.134 = f32[2,2,16,16,256]{4,3,2,1,0:T(8,128)} fusion(f32[2,2,16,16,256]{4,3,2,1,0:T(8,128)S(1)} %broadcast_select_fusion.5, f32[2,2,4,16,256]{4,3,2,1,0:T(8,128)S(1)} %collective-permute-done.7, f32[2,2,4,16,256]{4,3,2,1,0:T(8,128)S(1)} %collective-permute-done.6, f32[16,16,256]{2,1,0:T(8,128)S(1)} %copy-done.1, ...), kind=kLoop, calls=%fused_computation.359 | loop fusion | flops 13107200 | bytes 3932176 | tf_op jit(solution)/shard_map/add | solution.py:89
  102.0 6.8 %scatter-add.31 = f32[2,2,16,16,256]{4,3,2,1,0:T(8,128)} dynamic-update-slice(f32[2,2,16,16,256]{4,3,2,1,0:T(8,128)} %fusion.134, f32[2,2,16,16,1]{4,3,2,1,0:T(8,128)S(1)} %copy.262, s32[]{:T(128)} %constant.233.clone.1, s32[]{:T(128)} %constant.233.clone.1, s32[]{:T(128)} %constant.233.clone.1, s32[]{:T(128)} %constant.233.clone.1, s32[]{:T(128)} %constant.247.clone.1) | dynamic-update-slice | bytes 8196 | tf_op jit(solution)/shard_map/scatter-add | solution.py:98
  108.9 1.4 broadcast_select_fusion.4
  111.6 5.0 %collective-permute-start.9 = (f32[2,2,4,16,256]{4,3,2,1,0:T(8,128)S(1)}, f32[2,2,4,16,256]{4,3,2,1,0:T(8,128)S(1)}, u32[]{:S(2)}, u32[]{:S(2)}) collective-permute-start(f32[2,2,4,16,256]{4,3,2,1,0:T(8,128)S(1)} %get-tuple-element.129), channel_id=1, source_target_pairs={{0,1},{1,2},{2,3},{4,5},{5,6},{6,7},{8,9},{9,10},{10,11},{12,13},{... | collective-permute-start | bytes 786440 | tf_op jit(solution)/shard_map/ppermute | solution.py:21
  117.1 2.0 collective-permute-done.8
  119.0 1.5 collective-permute-done.9
  120.5 4.5 %fusion.108 = f32[2,2,16,16,256]{4,3,2,1,0:T(8,128)} fusion(f32[2,2,16,16,256]{4,3,2,1,0:T(8,128)S(1)} %broadcast_select_fusion.4, f32[2,2,4,16,256]{4,3,2,1,0:T(8,128)S(1)} %collective-permute-done.9, f32[2,2,4,16,256]{4,3,2,1,0:T(8,128)S(1)} %collective-permute-done.8, f32[16,16,256]{2,1,0:T(8,128)S(1)} %copy-done.1, ...), kind=kLoop, calls=%fused_computation.333 | loop fusion | flops 13107200 | bytes 3932176 | tf_op jit(solution)/shard_map/add | solution.py:89
  127.1 6.8 %scatter-add.34 = f32[2,2,16,16,256]{4,3,2,1,0:T(8,128)} dynamic-update-slice(f32[2,2,16,16,256]{4,3,2,1,0:T(8,128)} %fusion.108, f32[2,2,16,16,1]{4,3,2,1,0:T(8,128)S(1)} %copy.265, s32[]{:T(128)} %constant.233.clone.1, s32[]{:T(128)} %constant.233.clone.1, s32[]{:T(128)} %constant.233.clone.1, s32[]{:T(128)} %constant.233.clone.1, s32[]{:T(128)} %constant.247.clone.1) | dynamic-update-slice | bytes 8196 | tf_op jit(solution)/shard_map/scatter-add | solution.py:98
  134.0 1.4 broadcast_select_fusion.3
  136.7 5.0 %collective-permute-start.11 = (f32[2,2,4,16,256]{4,3,2,1,0:T(8,128)S(1)}, f32[2,2,4,16,256]{4,3,2,1,0:T(8,128)S(1)}, u32[]{:S(2)}, u32[]{:S(2)}) collective-permute-start(f32[2,2,4,16,256]{4,3,2,1,0:T(8,128)S(1)} %get-tuple-element.127), channel_id=1, source_target_pairs={{0,1},{1,2},{2,3},{4,5},{5,6},{6,7},{8,9},{9,10},{10,11},{12,13},{... | collective-permute-start | bytes 786440 | tf_op jit(solution)/shard_map/ppermute | solution.py:21
  142.1 2.0 collective-permute-done.10
  144.1 1.5 collective-permute-done.11
  145.6 4.5 %fusion.82 = f32[2,2,16,16,256]{4,3,2,1,0:T(8,128)} fusion(f32[2,2,16,16,256]{4,3,2,1,0:T(8,128)S(1)} %broadcast_select_fusion.3, f32[2,2,4,16,256]{4,3,2,1,0:T(8,128)S(1)} %collective-permute-done.11, f32[2,2,4,16,256]{4,3,2,1,0:T(8,128)S(1)} %collective-permute-done.10, f32[16,16,256]{2,1,0:T(8,128)S(1)} %copy-done.1, ...), kind=kLoop, calls=%fused_computation.307 | loop fusion | flops 13107200 | bytes 3932176 | tf_op jit(solution)/shard_map/add | solution.py:89
  152.2 6.8 %scatter-add.35 = f32[2,2,16,16,256]{4,3,2,1,0:T(8,128)} dynamic-update-slice(f32[2,2,16,16,256]{4,3,2,1,0:T(8,128)} %fusion.82, f32[2,2,16,16,1]{4,3,2,1,0:T(8,128)S(1)} %copy.268, s32[]{:T(128)} %constant.233.clone.1, s32[]{:T(128)} %constant.233.clone.1, s32[]{:T(128)} %constant.233.clone.1, s32[]{:T(128)} %constant.233.clone.1, s32[]{:T(128)} %constant.247.clone.1) | dynamic-update-slice | bytes 8196 | tf_op jit(solution)/shard_map/scatter-add | solution.py:98
  159.0 1.4 broadcast_select_fusion.2
  161.7 5.3 %collective-permute-start.13 = (f32[2,2,4,16,256]{4,3,2,1,0:T(8,128)S(1)}, f32[2,2,4,16,256]{4,3,2,1,0:T(8,128)S(1)}, u32[]{:S(2)}, u32[]{:S(2)}) collective-permute-start(f32[2,2,4,16,256]{4,3,2,1,0:T(8,128)S(1)} %get-tuple-element.125), channel_id=1, source_target_pairs={{0,1},{1,2},{2,3},{4,5},{5,6},{6,7},{8,9},{9,10},{10,11},{12,13},{... | collective-permute-start | bytes 786440 | tf_op jit(solution)/shard_map/ppermute | solution.py:21
  167.4 1.8 collective-permute-done.12
  169.2 1.5 collective-permute-done.13
  170.6 4.5 %fusion.56 = f32[2,2,16,16,256]{4,3,2,1,0:T(8,128)} fusion(f32[2,2,16,16,256]{4,3,2,1,0:T(8,128)S(1)} %broadcast_select_fusion.2, f32[2,2,4,16,256]{4,3,2,1,0:T(8,128)S(1)} %collective-permute-done.13, f32[2,2,4,16,256]{4,3,2,1,0:T(8,128)S(1)} %collective-permute-done.12, f32[16,16,256]{2,1,0:T(8,128)S(1)} %copy-done.1, ...), kind=kLoop, calls=%fused_computation.281 | loop fusion | flops 13107200 | bytes 3932176 | tf_op jit(solution)/shard_map/add | solution.py:89
  177.3 6.8 %scatter-add.36 = f32[2,2,16,16,256]{4,3,2,1,0:T(8,128)} dynamic-update-slice(f32[2,2,16,16,256]{4,3,2,1,0:T(8,128)} %fusion.56, f32[2,2,16,16,1]{4,3,2,1,0:T(8,128)S(1)} %copy.271, s32[]{:T(128)} %constant.233.clone.1, s32[]{:T(128)} %constant.233.clone.1, s32[]{:T(128)} %constant.233.clone.1, s32[]{:T(128)} %constant.233.clone.1, s32[]{:T(128)} %constant.247.clone.1) | dynamic-update-slice | bytes 8196 | tf_op jit(solution)/shard_map/scatter-add | solution.py:98
  184.1 1.4 broadcast_select_fusion.1
  186.8 5.0 %collective-permute-start.15 = (f32[2,2,4,16,256]{4,3,2,1,0:T(8,128)S(1)}, f32[2,2,4,16,256]{4,3,2,1,0:T(8,128)S(1)}, u32[]{:S(2)}, u32[]{:S(2)}) collective-permute-start(f32[2,2,4,16,256]{4,3,2,1,0:T(8,128)S(1)} %get-tuple-element.123), channel_id=1, source_target_pairs={{0,1},{1,2},{2,3},{4,5},{5,6},{6,7},{8,9},{9,10},{10,11},{12,13},{... | collective-permute-start | bytes 786440 | tf_op jit(solution)/shard_map/ppermute | solution.py:21
  192.3 2.0 collective-permute-done.14
  194.3 1.5 collective-permute-done.15
  195.7 4.5 %fusion.30 = f32[2,2,16,16,256]{4,3,2,1,0:T(8,128)} fusion(f32[2,2,16,16,256]{4,3,2,1,0:T(8,128)S(1)} %broadcast_select_fusion.1, f32[2,2,4,16,256]{4,3,2,1,0:T(8,128)S(1)} %collective-permute-done.15, f32[2,2,4,16,256]{4,3,2,1,0:T(8,128)S(1)} %collective-permute-done.14, f32[16,16,256]{2,1,0:T(8,128)S(1)} %copy-done.1, ...), kind=kLoop, calls=%fused_computation.255 | loop fusion | flops 13107200 | bytes 3932176 | tf_op jit(solution)/shard_map/add | solution.py:89
  202.3 6.7 %scatter-add.39 = f32[2,2,16,16,256]{4,3,2,1,0:T(8,128)} dynamic-update-slice(f32[2,2,16,16,256]{4,3,2,1,0:T(8,128)} %fusion.30, f32[2,2,16,16,1]{4,3,2,1,0:T(8,128)S(1)} %copy.274, s32[]{:T(128)} %constant.233.clone.1, s32[]{:T(128)} %constant.233.clone.1, s32[]{:T(128)} %constant.233.clone.1, s32[]{:T(128)} %constant.233.clone.1, s32[]{:T(128)} %constant.247.clone.1) | dynamic-update-slice | bytes 8196 | tf_op jit(solution)/shard_map/scatter-add | solution.py:98
  209.1 1.4 broadcast_select_fusion
  210.5 14.2 %collective-permute-done.16 = f32[2,2,16,16,256]{4,3,2,1,0:T(8,128)S(1)} collective-permute-done((f32[2,2,16,16,256]{4,3,2,1,0:T(8,128)S(1)}, f32[2,2,16,16,256]{4,3,2,1,0:T(8,128)S(1)}, u32[]{:S(2)}, u32[]{:S(2)}) %collective-permute-start.16) | collective-permute-done | bytes 1048608 | tf_op jit(solution)/shard_map/ppermute | solution.py:111
  224.7 1.7 collective-permute-start.18
  233.4 15.2 %collective-permute-done.17 = f32[2,2,16,16,256]{4,3,2,1,0:T(8,128)} collective-permute-done((f32[2,2,16,16,256]{4,3,2,1,0:T(8,128)S(1)}, f32[2,2,16,16,256]{4,3,2,1,0:T(8,128)}, u32[]{:S(2)}, u32[]{:S(2)}) %collective-permute-start.17) | collective-permute-done | bytes 1048608 | tf_op jit(solution)/shard_map/ppermute | solution.py:111
  250.2 1.3 constant_dynamic-update-slice_fusion.3
  252.3 1.8 fusion.1
  (160 shorter events, 49.5 us)
Async XLA Ops:
  0.6 13.7 %copy-start.9 = (f32[2,16,16,256]{3,2,1,0:T(8,128)S(1)}, f32[2,16,16,256]{3,2,1,0:T(8,128)}, u32[]{:S(2)}) copy-start(f32[2,16,16,256]{3,2,1,0:T(8,128)} %param.26) | copy-start | bytes 1572868
  0.6 13.7 %copy-start.8 = (f32[2,16,16,256]{3,2,1,0:T(8,128)S(1)}, f32[2,16,16,256]{3,2,1,0:T(8,128)}, u32[]{:S(2)}) copy-start(f32[2,16,16,256]{3,2,1,0:T(8,128)} %param.28) | copy-start | bytes 1572868
  0.7 9.5 %copy-start.14 = (f32[8,2]{0,1:T(2,128)S(1)}, f32[8,2]{0,1:T(2,128)}, u32[]{:S(2)}) copy-start(f32[8,2]{0,1:T(2,128)} %param.32) | copy-start | bytes 196
  0.7 9.8 %copy-start.15 = (f32[8,2,256]{2,1,0:T(2,128)S(1)}, f32[8,2,256]{2,1,0:T(2,128)}, u32[]{:S(2)}) copy-start(f32[8,2,256]{2,1,0:T(2,128)} %param.34) | copy-start | bytes 49156
  0.7 10.4 %copy-start.21 = (s32[2,256]{1,0:T(2,128)S(1)}, s32[2,256]{1,0:T(2,128)}, u32[]{:S(2)}) copy-start(s32[2,256]{1,0:T(2,128)} %param.33) | copy-start | bytes 6148
  0.7 11.4 %copy-start.20 = (s32[2]{0:T(128)S(1)}, s32[2]{0:T(128)}, u32[]{:S(2)}) copy-start(s32[2]{0:T(128)} %param.31) | copy-start | bytes 28
  1.9 11.3 %collective-permute-start = (f32[2,2,4,16,256]{4,3,2,1,0:T(8,128)S(1)}, f32[2,2,4,16,256]{4,3,2,1,0:T(8,128)S(1)}, u32[]{:S(2)}, u32[]{:S(2)}) collective-permute-start(f32[2,2,4,16,256]{4,3,2,1,0:T(8,128)S(1)} %get-tuple-element.138), channel_id=1, source_target_pairs={{1,0},{2,1},{3,2},{5,4},{6,5},{7,6},{9,8},{10,9},{11,10},{13,12},{... | collective-permute-start | bytes 786440 | tf_op jit(solution)/shard_map/ppermute | solution.py:23
  3.2 11.1 %collective-permute-start.1 = (f32[2,2,4,16,256]{4,3,2,1,0:T(8,128)S(1)}, f32[2,2,4,16,256]{4,3,2,1,0:T(8,128)S(1)}, u32[]{:S(2)}, u32[]{:S(2)}) collective-permute-start(f32[2,2,4,16,256]{4,3,2,1,0:T(8,128)S(1)} %get-tuple-element.139), channel_id=1, source_target_pairs={{0,1},{1,2},{2,3},{4,5},{5,6},{6,7},{8,9},{9,10},{10,11},{12,13},{... | collective-permute-start | bytes 786440 | tf_op jit(solution)/shard_map/ppermute | solution.py:21
  10.1 1.2 copy-start.25
  12.2 2.5 copy-start.1
  12.2 2.5 copy-start.11
  12.2 2.5 copy-start.12
  19.0 13.6 %copy-start.19 = (f32[2,256,1]{1,0,2:T(2,128)S(1)}, f32[2,256,1]{1,0,2:T(2,128)}, u32[]{:S(2)}) copy-start(f32[2,256,1]{1,0,2:T(2,128)} %get-tuple-element.145) | copy-start | bytes 6148
  19.0 13.6 %copy-start.22 = (s32[2,256]{1,0:T(2,128)S(1)}, s32[2,256]{1,0:T(2,128)}, u32[]{:S(2)}) copy-start(s32[2,256]{1,0:T(2,128)} %param.33) | copy-start | bytes 6148
  19.0 13.6 %copy-start.26 = (s32[256]{0:T(256)S(1)}, s32[256]{0:T(256)}, u32[]{:S(2)}) copy-start(s32[256]{0:T(256)} %copy-done.25) | copy-start | bytes 3076
  24.6 1.0 copy-start.10
  25.6 9.8 %collective-permute-start.2 = (f32[2,2,4,16,256]{4,3,2,1,0:T(8,128)S(1)}, f32[2,2,4,16,256]{4,3,2,1,0:T(8,128)S(1)}, u32[]{:S(2)}, u32[]{:S(2)}) collective-permute-start(f32[2,2,4,16,256]{4,3,2,1,0:T(8,128)S(1)} %get-tuple-element.134), channel_id=1, source_target_pairs={{1,0},{2,1},{3,2},{5,4},{6,5},{7,6},{9,8},{10,9},{11,10},{13,12},{... | collective-permute-start | bytes 786440 | tf_op jit(solution)/shard_map/ppermute | solution.py:23
  26.9 9.7 %collective-permute-start.3 = (f32[2,2,4,16,256]{4,3,2,1,0:T(8,128)S(1)}, f32[2,2,4,16,256]{4,3,2,1,0:T(8,128)}, u32[]{:S(2)}, u32[]{:S(2)}) collective-permute-start(f32[2,2,4,16,256]{4,3,2,1,0:T(8,128)S(1)} %get-tuple-element.135), channel_id=1, source_target_pairs={{0,1},{1,2},{2,3},{4,5},{5,6},{6,7},{8,9},{9,10},{10,11},{12,13},{... | collective-permute-start | bytes 786440 | tf_op jit(solution)/shard_map/ppermute | solution.py:21
  35.4 0.7 copy-start.13
  50.7 1.1 copy-start.6
  51.8 14.7 %copy-start.18 = (f32[2,256,1]{1,0,2:T(2,128)S(1)}, f32[2,256,1]{1,0,2:T(2,128)}, u32[]{:S(2)}) copy-start(f32[2,256,1]{1,0,2:T(2,128)} %get-tuple-element.144) | copy-start | bytes 6148
  51.8 14.7 %copy-start.23 = (s32[2,256]{1,0:T(2,128)S(1)}, s32[2,256]{1,0:T(2,128)}, u32[]{:S(2)}) copy-start(s32[2,256]{1,0:T(2,128)} %param.33) | copy-start | bytes 6148
  51.9 14.7 %copy-start.27 = (s32[256]{0:T(256)S(1)}, s32[256]{0:T(256)}, u32[]{:S(2)}) copy-start(s32[256]{0:T(256)} %copy-done.25) | copy-start | bytes 3076
  60.0 9.1 %collective-permute-start.4 = (f32[2,2,4,16,256]{4,3,2,1,0:T(8,128)S(1)}, f32[2,2,4,16,256]{4,3,2,1,0:T(8,128)S(1)}, u32[]{:S(2)}, u32[]{:S(2)}) collective-permute-start(f32[2,2,4,16,256]{4,3,2,1,0:T(8,128)S(1)} %get-tuple-element.132), channel_id=1, source_target_pairs={{1,0},{2,1},{3,2},{5,4},{6,5},{7,6},{9,8},{10,9},{11,10},{13,12},{... | collective-permute-start | bytes 786440 | tf_op jit(solution)/shard_map/ppermute | solution.py:23
  61.3 9.0 %collective-permute-start.5 = (f32[2,2,4,16,256]{4,3,2,1,0:T(8,128)S(1)}, f32[2,2,4,16,256]{4,3,2,1,0:T(8,128)S(1)}, u32[]{:S(2)}, u32[]{:S(2)}) collective-permute-start(f32[2,2,4,16,256]{4,3,2,1,0:T(8,128)S(1)} %get-tuple-element.133), channel_id=1, source_target_pairs={{0,1},{1,2},{2,3},{4,5},{5,6},{6,7},{8,9},{9,10},{10,11},{12,13},{... | collective-permute-start | bytes 786440 | tf_op jit(solution)/shard_map/ppermute | solution.py:21
  77.0 14.8 %copy-start.17 = (f32[2,256,1]{1,0,2:T(2,128)S(1)}, f32[2,256,1]{1,0,2:T(2,128)}, u32[]{:S(2)}) copy-start(f32[2,256,1]{1,0,2:T(2,128)} %get-tuple-element.143) | copy-start | bytes 6148
  77.0 18.4 %copy-start.7 = (f32[2,2,16,16,256]{4,3,2,1,0:T(8,128)S(1)}, f32[2,2,16,16,256]{4,3,2,1,0:T(8,128)}, u32[]{:S(2)}) copy-start(f32[2,2,16,16,256]{4,3,2,1,0:T(8,128)} %scatter-add.29) | copy-start | bytes 3145732
  85.2 8.7 %collective-permute-start.6 = (f32[2,2,4,16,256]{4,3,2,1,0:T(8,128)S(1)}, f32[2,2,4,16,256]{4,3,2,1,0:T(8,128)S(1)}, u32[]{:S(2)}, u32[]{:S(2)}) collective-permute-start(f32[2,2,4,16,256]{4,3,2,1,0:T(8,128)S(1)} %get-tuple-element.130), channel_id=1, source_target_pairs={{1,0},{2,1},{3,2},{5,4},{6,5},{7,6},{9,8},{10,9},{11,10},{13,12},{... | collective-permute-start | bytes 786440 | tf_op jit(solution)/shard_map/ppermute | solution.py:23
  86.5 8.9 %collective-permute-start.7 = (f32[2,2,4,16,256]{4,3,2,1,0:T(8,128)S(1)}, f32[2,2,4,16,256]{4,3,2,1,0:T(8,128)S(1)}, u32[]{:S(2)}, u32[]{:S(2)}) collective-permute-start(f32[2,2,4,16,256]{4,3,2,1,0:T(8,128)S(1)} %get-tuple-element.131), channel_id=1, source_target_pairs={{0,1},{1,2},{2,3},{4,5},{5,6},{6,7},{8,9},{9,10},{10,11},{12,13},{... | collective-permute-start | bytes 786440 | tf_op jit(solution)/shard_map/ppermute | solution.py:21
  102.0 14.6 %copy-start.16 = (f32[2,256,1]{1,0,2:T(2,128)S(1)}, f32[2,256,1]{1,0,2:T(2,128)}, u32[]{:S(2)}) copy-start(f32[2,256,1]{1,0,2:T(2,128)} %get-tuple-element.142) | copy-start | bytes 6148
  102.0 18.5 %copy-start.2 = (f32[2,2,16,16,256]{4,3,2,1,0:T(8,128)S(1)}, f32[2,2,16,16,256]{4,3,2,1,0:T(8,128)}, u32[]{:S(2)}) copy-start(f32[2,2,16,16,256]{4,3,2,1,0:T(8,128)} %scatter-add.30) | copy-start | bytes 3145732
  110.3 8.7 %collective-permute-start.8 = (f32[2,2,4,16,256]{4,3,2,1,0:T(8,128)S(1)}, f32[2,2,4,16,256]{4,3,2,1,0:T(8,128)S(1)}, u32[]{:S(2)}, u32[]{:S(2)}) collective-permute-start(f32[2,2,4,16,256]{4,3,2,1,0:T(8,128)S(1)} %get-tuple-element.128), channel_id=1, source_target_pairs={{1,0},{2,1},{3,2},{5,4},{6,5},{7,6},{9,8},{10,9},{11,10},{13,12},{... | collective-permute-start | bytes 786440 | tf_op jit(solution)/shard_map/ppermute | solution.py:23
  111.6 8.9 %collective-permute-start.9 = (f32[2,2,4,16,256]{4,3,2,1,0:T(8,128)S(1)}, f32[2,2,4,16,256]{4,3,2,1,0:T(8,128)S(1)}, u32[]{:S(2)}, u32[]{:S(2)}) collective-permute-start(f32[2,2,4,16,256]{4,3,2,1,0:T(8,128)S(1)} %get-tuple-element.129), channel_id=1, source_target_pairs={{0,1},{1,2},{2,3},{4,5},{5,6},{6,7},{8,9},{9,10},{10,11},{12,13},{... | collective-permute-start | bytes 786440 | tf_op jit(solution)/shard_map/ppermute | solution.py:21
  127.1 18.4 %copy-start.3 = (f32[2,2,16,16,256]{4,3,2,1,0:T(8,128)S(1)}, f32[2,2,16,16,256]{4,3,2,1,0:T(8,128)}, u32[]{:S(2)}) copy-start(f32[2,2,16,16,256]{4,3,2,1,0:T(8,128)} %scatter-add.31) | copy-start | bytes 3145732
  135.4 8.7 %collective-permute-start.10 = (f32[2,2,4,16,256]{4,3,2,1,0:T(8,128)S(1)}, f32[2,2,4,16,256]{4,3,2,1,0:T(8,128)S(1)}, u32[]{:S(2)}, u32[]{:S(2)}) collective-permute-start(f32[2,2,4,16,256]{4,3,2,1,0:T(8,128)S(1)} %get-tuple-element.126), channel_id=1, source_target_pairs={{1,0},{2,1},{3,2},{5,4},{6,5},{7,6},{9,8},{10,9},{11,10},{13,12},{... | collective-permute-start | bytes 786440 | tf_op jit(solution)/shard_map/ppermute | solution.py:23
  136.7 8.9 %collective-permute-start.11 = (f32[2,2,4,16,256]{4,3,2,1,0:T(8,128)S(1)}, f32[2,2,4,16,256]{4,3,2,1,0:T(8,128)S(1)}, u32[]{:S(2)}, u32[]{:S(2)}) collective-permute-start(f32[2,2,4,16,256]{4,3,2,1,0:T(8,128)S(1)} %get-tuple-element.127), channel_id=1, source_target_pairs={{0,1},{1,2},{2,3},{4,5},{5,6},{6,7},{8,9},{9,10},{10,11},{12,13},{... | collective-permute-start | bytes 786440 | tf_op jit(solution)/shard_map/ppermute | solution.py:21
  152.2 18.5 %copy-start.4 = (f32[2,2,16,16,256]{4,3,2,1,0:T(8,128)S(1)}, f32[2,2,16,16,256]{4,3,2,1,0:T(8,128)}, u32[]{:S(2)}) copy-start(f32[2,2,16,16,256]{4,3,2,1,0:T(8,128)} %scatter-add.34) | copy-start | bytes 3145732
  160.4 8.7 %collective-permute-start.12 = (f32[2,2,4,16,256]{4,3,2,1,0:T(8,128)S(1)}, f32[2,2,4,16,256]{4,3,2,1,0:T(8,128)S(1)}, u32[]{:S(2)}, u32[]{:S(2)}) collective-permute-start(f32[2,2,4,16,256]{4,3,2,1,0:T(8,128)S(1)} %get-tuple-element.124), channel_id=1, source_target_pairs={{1,0},{2,1},{3,2},{5,4},{6,5},{7,6},{9,8},{10,9},{11,10},{13,12},{... | collective-permute-start | bytes 786440 | tf_op jit(solution)/shard_map/ppermute | solution.py:23
  161.7 8.9 %collective-permute-start.13 = (f32[2,2,4,16,256]{4,3,2,1,0:T(8,128)S(1)}, f32[2,2,4,16,256]{4,3,2,1,0:T(8,128)S(1)}, u32[]{:S(2)}, u32[]{:S(2)}) collective-permute-start(f32[2,2,4,16,256]{4,3,2,1,0:T(8,128)S(1)} %get-tuple-element.125), channel_id=1, source_target_pairs={{0,1},{1,2},{2,3},{4,5},{5,6},{6,7},{8,9},{9,10},{10,11},{12,13},{... | collective-permute-start | bytes 786440 | tf_op jit(solution)/shard_map/ppermute | solution.py:21
  177.3 18.4 %copy-start.5 = (f32[2,2,16,16,256]{4,3,2,1,0:T(8,128)S(1)}, f32[2,2,16,16,256]{4,3,2,1,0:T(8,128)}, u32[]{:S(2)}) copy-start(f32[2,2,16,16,256]{4,3,2,1,0:T(8,128)} %scatter-add.35) | copy-start | bytes 3145732
  185.5 8.7 %collective-permute-start.14 = (f32[2,2,4,16,256]{4,3,2,1,0:T(8,128)S(1)}, f32[2,2,4,16,256]{4,3,2,1,0:T(8,128)S(1)}, u32[]{:S(2)}, u32[]{:S(2)}) collective-permute-start(f32[2,2,4,16,256]{4,3,2,1,0:T(8,128)S(1)} %get-tuple-element.122), channel_id=1, source_target_pairs={{1,0},{2,1},{3,2},{5,4},{6,5},{7,6},{9,8},{10,9},{11,10},{13,12},{... | collective-permute-start | bytes 786440 | tf_op jit(solution)/shard_map/ppermute | solution.py:23
  186.8 8.9 %collective-permute-start.15 = (f32[2,2,4,16,256]{4,3,2,1,0:T(8,128)S(1)}, f32[2,2,4,16,256]{4,3,2,1,0:T(8,128)S(1)}, u32[]{:S(2)}, u32[]{:S(2)}) collective-permute-start(f32[2,2,4,16,256]{4,3,2,1,0:T(8,128)S(1)} %get-tuple-element.123), channel_id=1, source_target_pairs={{0,1},{1,2},{2,3},{4,5},{5,6},{6,7},{8,9},{9,10},{10,11},{12,13},{... | collective-permute-start | bytes 786440 | tf_op jit(solution)/shard_map/ppermute | solution.py:21
  201.4 25.1 %copy-start.24 = (s32[8]{0:T(128)S(1)}, s32[8]{0:T(128)}, u32[]{:S(2)}) copy-start(s32[8]{0:T(128)} %param.35) | copy-start | bytes 100
  210.4 14.3 %collective-permute-start.16 = (f32[2,2,16,16,256]{4,3,2,1,0:T(8,128)S(1)}, f32[2,2,16,16,256]{4,3,2,1,0:T(8,128)S(1)}, u32[]{:S(2)}, u32[]{:S(2)}) collective-permute-start(f32[2,2,16,16,256]{4,3,2,1,0:T(8,128)S(1)} %broadcast_select_fusion), channel_id=1, source_target_pairs={{0,4},{4,8},{8,12},{12,0},{1,5},{5,9},{9,13},{13,1},{2,6},{6,10},{... | collective-permute-start | bytes 3145736 | tf_op jit(solution)/shard_map/ppermute | solution.py:111
  224.7 23.9 %collective-permute-start.17 = (f32[2,2,16,16,256]{4,3,2,1,0:T(8,128)S(1)}, f32[2,2,16,16,256]{4,3,2,1,0:T(8,128)}, u32[]{:S(2)}, u32[]{:S(2)}) collective-permute-start(f32[2,2,16,16,256]{4,3,2,1,0:T(8,128)S(1)} %collective-permute-done.16), channel_id=1, source_target_pairs={{0,4},{4,8},{8,12},{12,0},{1,5},{5,9},{9,13},{13,1},{2,6},{6,10},{... | collective-permute-start | bytes 3145736 | tf_op jit(solution)/shard_map/ppermute | solution.py:111
  224.7 25.4 %collective-permute-start.18 = (f32[2,2,16,16,256]{4,3,2,1,0:T(8,128)S(1)}, f32[2,2,16,16,256]{4,3,2,1,0:T(8,128)S(1)}, u32[]{:S(2)}, u32[]{:S(2)}) collective-permute-start(f32[2,2,16,16,256]{4,3,2,1,0:T(8,128)S(1)} %broadcast_select_fusion), channel_id=1, source_target_pairs={{0,12},{4,0},{8,4},{12,8},{1,13},{5,1},{9,5},{13,9},{2,14},{6,2},{... | collective-permute-start | bytes 3145736 | tf_op jit(solution)/shard_map/ppermute | solution.py:114
  233.4 16.6 %copy-start = (f32[2,2,16,16,256]{4,3,2,1,0:T(8,128)S(1)}, f32[2,2,16,16,256]{4,3,2,1,0:T(8,128)}, u32[]{:S(2)}) copy-start(f32[2,2,16,16,256]{4,3,2,1,0:T(8,128)} %scatter-add.39) | copy-start | bytes 3145732
